TPU v7x, 512 devices: a whole 4x4x16 slice. The times are simulated.
512 devices in a mesh: sub: 16 (over z), leaf: 32 (over y, x, core).
Axes of the slice: x: 4, y: 4, z: 16, core: 2. Of those that a mesh axis runs over, the one named last changes fastest.
Arguments:
- shift: float32 [1], replicated, may hold values from 0.5 to 2
- self_terms: float32 [524288], P(('leaf', 'sub')), may hold values from 1 to 2
- order: int32 [512, 1024], P(('leaf', 'sub')), may hold values from 0 to 1023, each once within a row
- split: int32 [512], P(('leaf', 'sub')), may hold values from 256 to 768
- coupling: bfloat16 [524288, 768], P(('leaf', 'sub')), as said below
- higher: bfloat16 [524288, 512], P(('leaf', 'sub'))
Outputs:
- applied_higher: bfloat16 [524288, 512], P(('leaf', 'sub'))
Inputs may be any that keep to these rules, and one draw needn't show every extreme that they name: `coupling`: at every node of every level, the symmetric matrix made of diag and the blocks U V^T and V U^T of this and lower levels is positive definite.
All inputs are finite; a program needn't handle non-finite values.
Results may differ from a plain program's by a relative error of at most 0.001.
The roundings to bfloat16 on the way count: a program that leaves them out, or rounds other values in their place, can miss the bound.
Values sent between devices are 32-bit elements; how exact they have to be, the bound alone decides.
A program may use at most 64 MiB of HBM per device.

v0:
```python
import jax
import jax.numpy as jnp
from jax import lax
from jax.sharding import PartitionSpec as P

RANK = 128


def from_partner(value, axis, stride):
    mask = 2**stride
    pairs = [(source, source ^ mask) for source in range(lax.axis_size(axis))]
    return lax.ppermute(value, axis, pairs)


def factor_solve(factor, target):
    lower_part = lax.linalg.triangular_solve(factor, target, left_side=True, lower=True)
    return lax.linalg.triangular_solve(
        factor, lower_part, left_side=True, lower=True, transpose_a=True
    )


def core_terms(left_sum, right_sum):
    width = left_sum.shape[0]
    first = left_sum[:, :width]
    projected = left_sum[:, width:]
    second = right_sum[:, :width]
    beyond = right_sum[:, width:]
    identity_block = jnp.eye(width, dtype=jnp.float32)
    first_factor = jnp.linalg.cholesky(first)
    first_inverse = factor_solve(first_factor, identity_block)
    schur_factor = jnp.linalg.cholesky(first_inverse - second)
    target = beyond - jnp.dot(second, projected, precision=lax.Precision.HIGHEST)
    back = factor_solve(schur_factor, target) - projected
    across = beyond + jnp.dot(second, back, precision=lax.Precision.HIGHEST)
    return (across, back)


def project_rows(basis, columns):
    return lax.dot_general(
        basis, columns, (((0,), (0,)), ((), ())), preferred_element_type=jnp.float32
    )


def node_step(columns, mine, other, is_left):
    left_sum = jnp.where(is_left, mine, other)
    right_sum = jnp.where(is_left, other, mine)
    across, back = core_terms(left_sum, right_sum)
    coefficient = jnp.where(is_left, -across, back).astype(jnp.bfloat16)
    update = columns[:, RANK:].astype(jnp.float32) + jnp.dot(
        columns[:, :RANK], coefficient, preferred_element_type=jnp.float32
    )
    return update.astype(jnp.bfloat16)


def per_device(shift, self_terms, order, split, coupling, higher):
    sub_bits = lax.axis_size("sub").bit_length() - 1
    diagonal = shift[0] + self_terms
    joined = jnp.concatenate([coupling, higher], axis=1).astype(jnp.float32)
    columns = (joined / diagonal[:, None]).astype(jnp.bfloat16)
    inside = (order[0] < split[0]).astype(jnp.bfloat16)[:, None]
    outside = 1 - inside
    basis = coupling[:, :RANK]
    left_sum = project_rows(basis * inside, columns)
    right_sum = project_rows(basis * outside, columns)
    across, back = core_terms(left_sum, right_sum)
    own = columns[:, :RANK]
    update = columns[:, RANK:].astype(jnp.float32)
    update = update + jnp.dot(
        own * inside, (-across).astype(jnp.bfloat16), preferred_element_type=jnp.float32
    )
    update = update + jnp.dot(
        own * outside, back.astype(jnp.bfloat16), preferred_element_type=jnp.float32
    )
    columns = update.astype(jnp.bfloat16)
    position = lax.axis_index("sub")
    for level in range(1, sub_bits + 1):
        basis = coupling[:, level * RANK : (level + 1) * RANK]
        partial_value = project_rows(basis, columns)
        stride = 2 ** (level - 1)
        mine = partial_value
        for bit in range(level - 1):
            mine = mine + from_partner(mine, "sub", bit)
        other = from_partner(mine, "sub", level - 1)
        is_left = position // stride % 2 == 0
        columns = node_step(columns, mine, other, is_left)
    top = sub_bits + 1
    basis = coupling[:, top * RANK : (top + 1) * RANK]
    partial_value = project_rows(basis, columns)
    mine = lax.psum(partial_value, "sub")
    other = from_partner(mine, "leaf", 0)
    is_left = lax.axis_index("leaf") % 2 == 0
    return node_step(columns, mine, other, is_left)


def solution(mesh):
    in_specs = (
        P(),
        P(("leaf", "sub")),
        P(("leaf", "sub"), None),
        P(("leaf", "sub")),
        P(("leaf", "sub"), None),
        P(("leaf", "sub"), None),
    )
    out_specs = P(("leaf", "sub"), None)
    return jax.shard_map(
        per_device, mesh=mesh, in_specs=in_specs, out_specs=out_specs, check_vma=False
    )
```

profile of v0, /device:TPU:1, one launch (start us, length us, event | category | flops | bytes accessed | tf_op | source)
XLA Modules:
  0.0 782.3 jit_solution(3534729396626597273)
XLA Ops:
  17.2 11.7 %cholesky.194 = f32[128,128]{1,0:T(8,128)S(1)} custom-call(f32[128,128]{1,0:T(8,128)S(1)} %fusion.114), custom_call_target="Cholesky" | custom-call | tf_op jit(solution)/shard_map/jit(cholesky)/cholesky | solution.py:29
  42.2 11.7 %cholesky.205 = f32[128,128]{1,0:T(8,128)S(1)} custom-call(f32[128,128]{1,0:T(8,128)S(1)} %fusion.111), custom_call_target="Cholesky" | custom-call | tf_op jit(solution)/shard_map/jit(cholesky)/cholesky | solution.py:31
  86.1 11.7 %cholesky.216 = f32[128,128]{1,0:T(8,128)S(1)} custom-call(f32[128,128]{1,0:T(8,128)S(1)} %fusion.107), custom_call_target="Cholesky" | custom-call | tf_op jit(solution)/shard_map/jit(cholesky)/cholesky | solution.py:29
  110.3 11.7 %cholesky.227 = f32[128,128]{1,0:T(8,128)S(1)} custom-call(f32[128,128]{1,0:T(8,128)S(1)} %fusion.104), custom_call_target="Cholesky" | custom-call | tf_op jit(solution)/shard_map/jit(cholesky)/cholesky | solution.py:31
  123.3 21.7 %custom-call.39 = f32[1,128,128]{1,2,0:T(8,128)S(1)} custom-call(f32[1,128,128]{2,1,0:T(8,128)S(1)} %fusion.64), custom_call_target="InvertDiagBlocksLowerTriangular" | custom-call | tf_op jit(solution)/shard_map/triangular_solve | solution.py:17
  162.2 12.1 %collective-permute-start.2 = (f32[128,1024]{0,1:T(8,128)S(1)}, f32[128,1024]{0,1:T(8,128)}, u32[]{:S(2)}, u32[]{:S(2)}) collective-permute-start(f32[128,1024]{0,1:T(8,128)S(1)} %add.127), channel_id=1, source_target_pairs={{0,64},{32,96},{64,0},{96,32},{128,192},{160,224},{192,128},{224,1... | collective-permute-start | bytes 1572872 | tf_op jit(solution)/shard_map/ppermute | solution.py:12
  174.4 22.8 %collective-permute-done.2 = f32[128,1024]{0,1:T(8,128)} collective-permute-done((f32[128,1024]{0,1:T(8,128)S(1)}, f32[128,1024]{0,1:T(8,128)}, u32[]{:S(2)}, u32[]{:S(2)}) %collective-permute-start.2) | collective-permute-done | bytes 524320 | tf_op jit(solution)/shard_map/ppermute | solution.py:12
  198.5 11.7 %cholesky.238 = f32[128,128]{1,0:T(8,128)S(1)} custom-call(f32[128,128]{1,0:T(8,128)S(1)} %fusion.100), custom_call_target="Cholesky" | custom-call | tf_op jit(solution)/shard_map/jit(cholesky)/cholesky | solution.py:29
  222.6 11.7 %cholesky.249 = f32[128,128]{1,0:T(8,128)S(1)} custom-call(f32[128,128]{1,0:T(8,128)S(1)} %fusion.97), custom_call_target="Cholesky" | custom-call | tf_op jit(solution)/shard_map/jit(cholesky)/cholesky | solution.py:31
  269.3 19.9 %collective-permute-done.4 = f32[128,896]{0,1:T(8,128)S(1)} collective-permute-done((f32[128,896]{0,1:T(8,128)S(1)}, f32[128,896]{0,1:T(8,128)S(1)}, u32[]{:S(2)}, u32[]{:S(2)}) %collective-permute-start.4) | collective-permute-done | bytes 458784 | tf_op jit(solution)/shard_map/ppermute | solution.py:12
  298.1 39.4 %collective-permute-done.5 = f32[128,896]{0,1:T(8,128)S(1)} collective-permute-done((f32[128,896]{0,1:T(8,128)S(1)}, f32[128,896]{0,1:T(8,128)S(1)}, u32[]{:S(2)}, u32[]{:S(2)}) %collective-permute-start.5) | collective-permute-done | bytes 458784 | tf_op jit(solution)/shard_map/ppermute | solution.py:12
  337.7 11.7 %cholesky.260 = f32[128,128]{1,0:T(8,128)S(1)} custom-call(f32[128,128]{1,0:T(8,128)S(1)} %fusion.93), custom_call_target="Cholesky" | custom-call | tf_op jit(solution)/shard_map/jit(cholesky)/cholesky | solution.py:29
  361.7 11.7 %cholesky.271 = f32[128,128]{1,0:T(8,128)S(1)} custom-call(f32[128,128]{1,0:T(8,128)S(1)} %fusion.90), custom_call_target="Cholesky" | custom-call | tf_op jit(solution)/shard_map/jit(cholesky)/cholesky | solution.py:31
  403.3 20.3 %collective-permute-done.7 = f32[128,768]{0,1:T(8,128)S(1)} collective-permute-done((f32[128,768]{0,1:T(8,128)S(1)}, f32[128,768]{0,1:T(8,128)S(1)}, u32[]{:S(2)}, u32[]{:S(2)}) %collective-permute-start.7) | collective-permute-done | bytes 393248 | tf_op jit(solution)/shard_map/ppermute | solution.py:12
  428.0 35.9 %collective-permute-done.8 = f32[128,768]{0,1:T(8,128)S(1)} collective-permute-done((f32[128,768]{0,1:T(8,128)S(1)}, f32[128,768]{0,1:T(8,128)S(1)}, u32[]{:S(2)}, u32[]{:S(2)}) %collective-permute-start.8) | collective-permute-done | bytes 393248 | tf_op jit(solution)/shard_map/ppermute | solution.py:12
  464.7 19.0 %collective-permute-start.9 = (f32[128,768]{0,1:T(8,128)}, f32[128,768]{0,1:T(8,128)}, u32[]{:S(2)}, u32[]{:S(2)}) collective-permute-start(f32[128,768]{0,1:T(8,128)} %add.138), channel_id=1, source_target_pairs={{0,256},{32,288},{64,320},{96,352},{128,384},{160,416},{192,448},{... | collective-permute-start | bytes 1179656 | tf_op jit(solution)/shard_map/ppermute | solution.py:12
  483.7 14.6 %collective-permute-done.9 = f32[128,768]{0,1:T(8,128)} collective-permute-done((f32[128,768]{0,1:T(8,128)}, f32[128,768]{0,1:T(8,128)}, u32[]{:S(2)}, u32[]{:S(2)}) %collective-permute-start.9) | collective-permute-done | bytes 393248 | tf_op jit(solution)/shard_map/ppermute | solution.py:12
  503.9 13.2 %cholesky.282 = f32[128,128]{1,0:T(8,128)} custom-call(f32[128,128]{1,0:T(8,128)} %fusion.86), custom_call_target="Cholesky" | custom-call | tf_op jit(solution)/shard_map/jit(cholesky)/cholesky | solution.py:29
  540.1 13.2 %cholesky.293 = f32[128,128]{1,0:T(8,128)} custom-call(f32[128,128]{1,0:T(8,128)} %fusion.83), custom_call_target="Cholesky" | custom-call | tf_op jit(solution)/shard_map/jit(cholesky)/cholesky | solution.py:31
  556.9 11.4 %custom-call.42 = f32[1,128,128]{1,2,0:T(8,128)} custom-call(f32[1,128,128]{2,1,0:T(8,128)} %fusion.70), custom_call_target="InvertDiagBlocksLowerTriangular" | custom-call | tf_op jit(solution)/shard_map/triangular_solve | solution.py:17
  575.8 133.2 %all-reduce.2.cloned.1.call-done = f32[128,640]{0,1:T(8,128)} async-done(((f32[128,640]{0,1:T(8,128)}), f32[128,640]{0,1:T(8,128)}) %all-reduce.2.cloned.1.call-update) | async-done | bytes 327696 | tf_op jit(solution)/shard_map/psum | solution.py:89
  708.9 12.3 %collective-permute-start.10 = (f32[128,640]{0,1:T(8,128)}, f32[128,640]{0,1:T(8,128)S(1)}, u32[]{:S(2)}, u32[]{:S(2)}) collective-permute-start(f32[128,640]{0,1:T(8,128)} %all-reduce.2.cloned.1.call-done), channel_id=1, source_target_pairs={{0,1},{1,0},{2,3},{3,2},{4,5},{5,4},{6,7},{7,6},{8,9},{9,8},{10,11... | collective-permute-start | bytes 983048 | tf_op jit(solution)/shard_map/ppermute | solution.py:12
  723.9 11.7 %cholesky.304 = f32[128,128]{1,0:T(8,128)S(1)} custom-call(f32[128,128]{1,0:T(8,128)S(1)} %fusion.79), custom_call_target="Cholesky" | custom-call | tf_op jit(solution)/shard_map/jit(cholesky)/cholesky | solution.py:29
  747.8 11.7 %cholesky.315 = f32[128,128]{1,0:T(8,128)S(1)} custom-call(f32[128,128]{1,0:T(8,128)S(1)} %fusion.76), custom_call_target="Cholesky" | custom-call | tf_op jit(solution)/shard_map/jit(cholesky)/cholesky | solution.py:31
  (170 shorter events, 260.0 us)
Async XLA Ops:
  6.5 702.4 %all-reduce.2.cloned.1.call-start = ((), (), s32[]{:S(2)}) async-start(), calls=%async_computation | async-start | bytes 655360 | tf_op jit(solution)/shard_map/psum | solution.py:89
  14.8 0.8 copy-start.5
  71.0 2.0 copy-start
  73.0 12.9 %collective-permute-start = (f32[128,1152]{0,1:T(8,128)S(1)}, f32[128,1152]{0,1:T(8,128)S(1)}, u32[]{:S(2)}, u32[]{:S(2)}) collective-permute-start(f32[128,1152]{0,1:T(8,128)S(1)} %convolution_bitcast_fusion), channel_id=1, source_target_pairs={{0,32},{32,0},{64,96},{96,64},{128,160},{160,128},{192,224},{224,1... | collective-permute-start | bytes 1769480 | tf_op jit(solution)/shard_map/ppermute | solution.py:12
  146.7 3.0 copy-start.1
  149.7 1.4 copy-start.2
  151.0 11.1 %collective-permute-start.1 = (f32[128,1024]{0,1:T(8,128)S(1)}, f32[128,1024]{0,1:T(8,128)S(1)}, u32[]{:S(2)}, u32[]{:S(2)}) collective-permute-start(f32[128,1024]{0,1:T(8,128)S(1)} %convolution_bitcast_fusion.1), channel_id=1, source_target_pairs={{0,32},{32,0},{64,96},{96,64},{128,160},{160,128},{192,224},{224,1... | collective-permute-start | bytes 1572872 | tf_op jit(solution)/shard_map/ppermute | solution.py:12
  162.2 35.0 %collective-permute-start.2 = (f32[128,1024]{0,1:T(8,128)S(1)}, f32[128,1024]{0,1:T(8,128)}, u32[]{:S(2)}, u32[]{:S(2)}) collective-permute-start(f32[128,1024]{0,1:T(8,128)S(1)} %add.127), channel_id=1, source_target_pairs={{0,64},{32,96},{64,0},{96,32},{128,192},{160,224},{192,128},{224,1... | collective-permute-start | bytes 1572872 | tf_op jit(solution)/shard_map/ppermute | solution.py:12
  250.2 39.1 %copy-start.3 = (bf16[1024,896]{1,0:T(8,128)(2,1)}, bf16[1024,896]{1,0:T(8,128)(2,1)S(1)}, u32[]{:S(2)}) copy-start(bf16[1024,896]{1,0:T(8,128)(2,1)S(1)} %add_convert_fusion.1) | copy-start | bytes 5505028
  250.9 12.7 %collective-permute-start.3 = (f32[128,896]{0,1:T(8,128)S(1)}, f32[128,896]{0,1:T(8,128)S(1)}, u32[]{:S(2)}, u32[]{:S(2)}) collective-permute-start(f32[128,896]{0,1:T(8,128)S(1)} %convolution_bitcast_fusion.2), channel_id=1, source_target_pairs={{0,32},{32,0},{64,96},{96,64},{128,160},{160,128},{192,224},{224,1... | collective-permute-start | bytes 1376264 | tf_op jit(solution)/shard_map/ppermute | solution.py:12
  263.6 25.6 %collective-permute-start.4 = (f32[128,896]{0,1:T(8,128)S(1)}, f32[128,896]{0,1:T(8,128)S(1)}, u32[]{:S(2)}, u32[]{:S(2)}) collective-permute-start(f32[128,896]{0,1:T(8,128)S(1)} %add.131), channel_id=1, source_target_pairs={{0,64},{32,96},{64,0},{96,32},{128,192},{160,224},{192,128},{224,1... | collective-permute-start | bytes 1376264 | tf_op jit(solution)/shard_map/ppermute | solution.py:12
  289.3 48.2 %collective-permute-start.5 = (f32[128,896]{0,1:T(8,128)S(1)}, f32[128,896]{0,1:T(8,128)S(1)}, u32[]{:S(2)}, u32[]{:S(2)}) collective-permute-start(f32[128,896]{0,1:T(8,128)S(1)} %add.132), channel_id=1, source_target_pairs={{0,128},{32,160},{64,192},{96,224},{128,0},{160,32},{192,64},{224,... | collective-permute-start | bytes 1376264 | tf_op jit(solution)/shard_map/ppermute | solution.py:12
  389.2 12.1 %collective-permute-start.6 = (f32[128,768]{0,1:T(8,128)S(1)}, f32[128,768]{0,1:T(8,128)S(1)}, u32[]{:S(2)}, u32[]{:S(2)}) collective-permute-start(f32[128,768]{0,1:T(8,128)S(1)} %convolution_bitcast_fusion.3), channel_id=1, source_target_pairs={{0,32},{32,0},{64,96},{96,64},{128,160},{160,128},{192,224},{224,1... | collective-permute-start | bytes 1179656 | tf_op jit(solution)/shard_map/ppermute | solution.py:12
  401.4 22.2 %collective-permute-start.7 = (f32[128,768]{0,1:T(8,128)S(1)}, f32[128,768]{0,1:T(8,128)S(1)}, u32[]{:S(2)}, u32[]{:S(2)}) collective-permute-start(f32[128,768]{0,1:T(8,128)S(1)} %add.136), channel_id=1, source_target_pairs={{0,64},{32,96},{64,0},{96,32},{128,192},{160,224},{192,128},{224,1... | collective-permute-start | bytes 1179656 | tf_op jit(solution)/shard_map/ppermute | solution.py:12
  423.7 40.2 %collective-permute-start.8 = (f32[128,768]{0,1:T(8,128)S(1)}, f32[128,768]{0,1:T(8,128)S(1)}, u32[]{:S(2)}, u32[]{:S(2)}) collective-permute-start(f32[128,768]{0,1:T(8,128)S(1)} %add.137), channel_id=1, source_target_pairs={{0,128},{32,160},{64,192},{96,224},{128,0},{160,32},{192,64},{224,... | collective-permute-start | bytes 1179656 | tf_op jit(solution)/shard_map/ppermute | solution.py:12
  464.7 33.7 %collective-permute-start.9 = (f32[128,768]{0,1:T(8,128)}, f32[128,768]{0,1:T(8,128)}, u32[]{:S(2)}, u32[]{:S(2)}) collective-permute-start(f32[128,768]{0,1:T(8,128)} %add.138), channel_id=1, source_target_pairs={{0,256},{32,288},{64,320},{96,352},{128,384},{160,416},{192,448},{... | collective-permute-start | bytes 1179656 | tf_op jit(solution)/shard_map/ppermute | solution.py:12
  573.4 1.1 copy-start.4
  708.9 13.8 %collective-permute-start.10 = (f32[128,640]{0,1:T(8,128)}, f32[128,640]{0,1:T(8,128)S(1)}, u32[]{:S(2)}, u32[]{:S(2)}) collective-permute-start(f32[128,640]{0,1:T(8,128)} %all-reduce.2.cloned.1.call-done), channel_id=1, source_target_pairs={{0,1},{1,0},{2,3},{3,2},{4,5},{5,4},{6,7},{7,6},{8,9},{9,8},{10,11... | collective-permute-start | bytes 983048 | tf_op jit(solution)/shard_map/ppermute | solution.py:12
Sparse Core Ops, SparseCore 0:
  575.9 133.0 all-reduce.1
where the time goes:
time: 793 us; the launch traced here: 782 us
  waiting for transfers between devices  323 us (41%)
  other arithmetic  310 us (39%)
  starting transfers between devices  77.5 us (10%)
  matrix products  48.2 us (6%)
  between operations  16.1 us (2%)
    ppermute x11, waiting for transfers between devices, from_partner(): return lax.ppermute(value, axis, pairs)  190 us
    another operation x24, other arithmetic, factor_solve(): lax.linalg.triangular_solve(factor, lower_part, left_side=True, lower=Tru...  144 us
    psum x1, waiting for transfers between devices, per_device(): mine = lax.psum(partial_value, 'sub')  133 us
    ppermute x11, starting transfers between devices, from_partner(): return lax.ppermute(value, axis, pairs)  77.5 us
    another operation x18, other arithmetic, core_terms(): schur_factor = jnp.linalg.cholesky(first_inverse - second)  76.9 us
    another operation x18, other arithmetic, core_terms(): first_factor = jnp.linalg.cholesky(first)  76.6 us
  transfers between devices with their start and end apart: 12, of which 12 were waited for; matrix products, arithmetic and copies ran while one was open for 0% of the time, Pallas kernels for 0%

commit v1 on v0

--- a/solution.py
+++ b/solution.py
@@ -86,7 +86,9 @@
     top = sub_bits + 1
     basis = coupling[:, top * RANK : (top + 1) * RANK]
     partial_value = project_rows(basis, columns)
-    mine = lax.psum(partial_value, "sub")
+    mine = partial_value
+    for hop in (1, 2, 4, 8):
+        mine = mine + lax.ppermute(mine, "sub", [(dev, dev ^ hop) for dev in range(16)])
     other = from_partner(mine, "leaf", 0)
     is_left = lax.axis_index("leaf") % 2 == 0
     return node_step(columns, mine, other, is_left)

time: 793 us -> 741 us (0.934)
  waiting for transfers between devices: 323 us -> 261 us
  starting transfers between devices: 77.5 us -> 103 us
  between operations: 16.1 us -> 2.81 us
    psum x1 -> x0, waiting for transfers between devices: 133 us -> none  [per_device(): mine = lax.psum(partial_value, 'sub')]
    ppermute x0 -> x4, waiting for transfers between devices: none -> 71.6 us  [per_device(): lax.ppermute(mine, 'sub', [(dev, dev ^ hop) for dev in range(16)])]
    ppermute x0 -> x4, starting transfers between devices: none -> 35 us  [per_device(): lax.ppermute(mine, 'sub', [(dev, dev ^ hop) for dev in range(16)])]
    ppermute x11, starting transfers between devices: 77.5 us -> 67.6 us  [from_partner(): return lax.ppermute(value, axis, pairs)]
  transfers between devices with their start and end apart: 12 -> 15, of which waited for: 12 -> 15; matrix products, arithmetic and copies ran while one was open for 0% -> 0% of each run, Pallas kernels for 0% -> 0%
where the time goes in v1:
time: 741 us; the launch traced here: 730 us
  other arithmetic  309 us (42%)
  waiting for transfers between devices  261 us (35%)
  starting transfers between devices  103 us (14%)
  matrix products  47.4 us (6%)
    ppermute x11, waiting for transfers between devices, from_partner(): return lax.ppermute(value, axis, pairs)  190 us
    another operation x24, other arithmetic, factor_solve(): lax.linalg.triangular_solve(factor, lower_part, left_side=True, lower=Tru...  144 us
    another operation x18, other arithmetic, core_terms(): schur_factor = jnp.linalg.cholesky(first_inverse - second)  76.9 us
    another operation x18, other arithmetic, core_terms(): first_factor = jnp.linalg.cholesky(first)  76.6 us
    ppermute x4, waiting for transfers between devices, per_device(): lax.ppermute(mine, 'sub', [(dev, dev ^ hop) for dev in range(16)])  71.6 us
    ppermute x11, starting transfers between devices, from_partner(): return lax.ppermute(value, axis, pairs)  67.6 us
    ppermute x4, starting transfers between devices, per_device(): lax.ppermute(mine, 'sub', [(dev, dev ^ hop) for dev in range(16)])  35 us
  transfers between devices with their start and end apart: 15, of which 15 were waited for; matrix products, arithmetic and copies ran while one was open for 0% of the time, Pallas kernels for 0%

profile of v1, /device:TPU:1, one launch (start us, length us, event | category | flops | bytes accessed | tf_op | source)
XLA Modules:
  0.0 729.9 jit_solution(16292803775629360774)
XLA Ops:
  10.6 11.7 %cholesky.194 = f32[128,128]{1,0:T(8,128)S(1)} custom-call(f32[128,128]{1,0:T(8,128)S(1)} %fusion.114), custom_call_target="Cholesky" | custom-call | tf_op jit(solution)/shard_map/jit(cholesky)/cholesky | solution.py:29
  35.7 11.7 %cholesky.205 = f32[128,128]{1,0:T(8,128)S(1)} custom-call(f32[128,128]{1,0:T(8,128)S(1)} %fusion.111), custom_call_target="Cholesky" | custom-call | tf_op jit(solution)/shard_map/jit(cholesky)/cholesky | solution.py:31
  79.6 11.7 %cholesky.216 = f32[128,128]{1,0:T(8,128)S(1)} custom-call(f32[128,128]{1,0:T(8,128)S(1)} %fusion.107), custom_call_target="Cholesky" | custom-call | tf_op jit(solution)/shard_map/jit(cholesky)/cholesky | solution.py:29
  103.8 11.7 %cholesky.227 = f32[128,128]{1,0:T(8,128)S(1)} custom-call(f32[128,128]{1,0:T(8,128)S(1)} %fusion.104), custom_call_target="Cholesky" | custom-call | tf_op jit(solution)/shard_map/jit(cholesky)/cholesky | solution.py:31
  116.8 21.7 %custom-call.39 = f32[1,128,128]{1,2,0:T(8,128)S(1)} custom-call(f32[1,128,128]{2,1,0:T(8,128)S(1)} %fusion.64), custom_call_target="InvertDiagBlocksLowerTriangular" | custom-call | tf_op jit(solution)/shard_map/triangular_solve | solution.py:17
  155.7 12.2 %collective-permute-start.2 = (f32[128,1024]{0,1:T(8,128)S(1)}, f32[128,1024]{0,1:T(8,128)}, u32[]{:S(2)}, u32[]{:S(2)}) collective-permute-start(f32[128,1024]{0,1:T(8,128)S(1)} %add.137), channel_id=1, source_target_pairs={{0,64},{32,96},{64,0},{96,32},{128,192},{160,224},{192,128},{224,1... | collective-permute-start | bytes 1572872 | tf_op jit(solution)/shard_map/ppermute | solution.py:12
  167.9 22.9 %collective-permute-done.2 = f32[128,1024]{0,1:T(8,128)} collective-permute-done((f32[128,1024]{0,1:T(8,128)S(1)}, f32[128,1024]{0,1:T(8,128)}, u32[]{:S(2)}, u32[]{:S(2)}) %collective-permute-start.2) | collective-permute-done | bytes 524320 | tf_op jit(solution)/shard_map/ppermute | solution.py:12
  192.0 11.7 %cholesky.238 = f32[128,128]{1,0:T(8,128)S(1)} custom-call(f32[128,128]{1,0:T(8,128)S(1)} %fusion.100), custom_call_target="Cholesky" | custom-call | tf_op jit(solution)/shard_map/jit(cholesky)/cholesky | solution.py:29
  216.1 11.7 %cholesky.249 = f32[128,128]{1,0:T(8,128)S(1)} custom-call(f32[128,128]{1,0:T(8,128)S(1)} %fusion.97), custom_call_target="Cholesky" | custom-call | tf_op jit(solution)/shard_map/jit(cholesky)/cholesky | solution.py:31
  262.7 19.9 %collective-permute-done.4 = f32[128,896]{0,1:T(8,128)S(1)} collective-permute-done((f32[128,896]{0,1:T(8,128)S(1)}, f32[128,896]{0,1:T(8,128)S(1)}, u32[]{:S(2)}, u32[]{:S(2)}) %collective-permute-start.4) | collective-permute-done | bytes 458784 | tf_op jit(solution)/shard_map/ppermute | solution.py:12
  291.5 39.4 %collective-permute-done.5 = f32[128,896]{0,1:T(8,128)S(1)} collective-permute-done((f32[128,896]{0,1:T(8,128)S(1)}, f32[128,896]{0,1:T(8,128)S(1)}, u32[]{:S(2)}, u32[]{:S(2)}) %collective-permute-start.5) | collective-permute-done | bytes 458784 | tf_op jit(solution)/shard_map/ppermute | solution.py:12
  331.1 11.7 %cholesky.260 = f32[128,128]{1,0:T(8,128)S(1)} custom-call(f32[128,128]{1,0:T(8,128)S(1)} %fusion.93), custom_call_target="Cholesky" | custom-call | tf_op jit(solution)/shard_map/jit(cholesky)/cholesky | solution.py:29
  355.2 11.7 %cholesky.271 = f32[128,128]{1,0:T(8,128)S(1)} custom-call(f32[128,128]{1,0:T(8,128)S(1)} %fusion.90), custom_call_target="Cholesky" | custom-call | tf_op jit(solution)/shard_map/jit(cholesky)/cholesky | solution.py:31
  396.7 20.3 %collective-permute-done.7 = f32[128,768]{0,1:T(8,128)S(1)} collective-permute-done((f32[128,768]{0,1:T(8,128)S(1)}, f32[128,768]{0,1:T(8,128)S(1)}, u32[]{:S(2)}, u32[]{:S(2)}) %collective-permute-start.7) | collective-permute-done | bytes 393248 | tf_op jit(solution)/shard_map/ppermute | solution.py:12
  421.5 35.9 %collective-permute-done.8 = f32[128,768]{0,1:T(8,128)S(1)} collective-permute-done((f32[128,768]{0,1:T(8,128)S(1)}, f32[128,768]{0,1:T(8,128)S(1)}, u32[]{:S(2)}, u32[]{:S(2)}) %collective-permute-start.8) | collective-permute-done | bytes 393248 | tf_op jit(solution)/shard_map/ppermute | solution.py:12
  458.1 19.2 %collective-permute-start.9 = (f32[128,768]{0,1:T(8,128)}, f32[128,768]{0,1:T(8,128)}, u32[]{:S(2)}, u32[]{:S(2)}) collective-permute-start(f32[128,768]{0,1:T(8,128)} %add.148), channel_id=1, source_target_pairs={{0,256},{32,288},{64,320},{96,352},{128,384},{160,416},{192,448},{... | collective-permute-start | bytes 1179656 | tf_op jit(solution)/shard_map/ppermute | solution.py:12
  477.3 14.7 %collective-permute-done.9 = f32[128,768]{0,1:T(8,128)} collective-permute-done((f32[128,768]{0,1:T(8,128)}, f32[128,768]{0,1:T(8,128)}, u32[]{:S(2)}, u32[]{:S(2)}) %collective-permute-start.9) | collective-permute-done | bytes 393248 | tf_op jit(solution)/shard_map/ppermute | solution.py:12
  497.6 13.2 %cholesky.282 = f32[128,128]{1,0:T(8,128)} custom-call(f32[128,128]{1,0:T(8,128)} %fusion.86), custom_call_target="Cholesky" | custom-call | tf_op jit(solution)/shard_map/jit(cholesky)/cholesky | solution.py:29
  533.7 13.2 %cholesky.293 = f32[128,128]{1,0:T(8,128)} custom-call(f32[128,128]{1,0:T(8,128)} %fusion.83), custom_call_target="Cholesky" | custom-call | tf_op jit(solution)/shard_map/jit(cholesky)/cholesky | solution.py:31
  588.0 14.3 %collective-permute-done.11 = f32[128,640]{0,1:T(8,128)S(1)} collective-permute-done((f32[128,640]{0,1:T(8,128)S(1)}, f32[128,640]{0,1:T(8,128)S(1)}, u32[]{:S(2)}, u32[]{:S(2)}) %collective-permute-start.11) | collective-permute-done | bytes 327712 | tf_op jit(solution)/shard_map/ppermute | solution.py:91
  609.2 28.6 %collective-permute-done.12 = f32[128,640]{0,1:T(8,128)S(1)} collective-permute-done((f32[128,640]{0,1:T(8,128)S(1)}, f32[128,640]{0,1:T(8,128)S(1)}, u32[]{:S(2)}, u32[]{:S(2)}) %collective-permute-start.12) | collective-permute-done | bytes 327712 | tf_op jit(solution)/shard_map/ppermute | solution.py:91
  637.9 16.5 %collective-permute-start.13 = (f32[128,640]{0,1:T(8,128)S(1)}, f32[128,640]{0,1:T(8,128)S(1)}, u32[]{:S(2)}, u32[]{:S(2)}) collective-permute-start(f32[128,640]{0,1:T(8,128)S(1)} %add.154), channel_id=1, source_target_pairs={{0,256},{32,288},{64,320},{96,352},{128,384},{160,416},{192,448},{... | collective-permute-start | bytes 983048 | tf_op jit(solution)/shard_map/ppermute | solution.py:91
  654.4 20.1 %collective-permute-done.13 = f32[128,640]{0,1:T(8,128)S(1)} collective-permute-done((f32[128,640]{0,1:T(8,128)S(1)}, f32[128,640]{0,1:T(8,128)S(1)}, u32[]{:S(2)}, u32[]{:S(2)}) %collective-permute-start.13) | collective-permute-done | bytes 327712 | tf_op jit(solution)/shard_map/ppermute | solution.py:91
  678.3 11.7 %cholesky.304 = f32[128,128]{1,0:T(8,128)S(1)} custom-call(f32[128,128]{1,0:T(8,128)S(1)} %fusion.79), custom_call_target="Cholesky" | custom-call | tf_op jit(solution)/shard_map/jit(cholesky)/cholesky | solution.py:29
  (179 shorter events, 309.8 us)
Async XLA Ops:
  8.2 0.8 copy-start.5
  64.5 2.0 copy-start
  66.5 12.9 %collective-permute-start = (f32[128,1152]{0,1:T(8,128)S(1)}, f32[128,1152]{0,1:T(8,128)S(1)}, u32[]{:S(2)}, u32[]{:S(2)}) collective-permute-start(f32[128,1152]{0,1:T(8,128)S(1)} %convolution_bitcast_fusion), channel_id=1, source_target_pairs={{0,32},{32,0},{64,96},{96,64},{128,160},{160,128},{192,224},{224,1... | collective-permute-start | bytes 1769480 | tf_op jit(solution)/shard_map/ppermute | solution.py:12
  140.1 3.0 copy-start.1
  143.2 1.4 copy-start.2
  144.5 11.1 %collective-permute-start.1 = (f32[128,1024]{0,1:T(8,128)S(1)}, f32[128,1024]{0,1:T(8,128)S(1)}, u32[]{:S(2)}, u32[]{:S(2)}) collective-permute-start(f32[128,1024]{0,1:T(8,128)S(1)} %convolution_bitcast_fusion.1), channel_id=1, source_target_pairs={{0,32},{32,0},{64,96},{96,64},{128,160},{160,128},{192,224},{224,1... | collective-permute-start | bytes 1572872 | tf_op jit(solution)/shard_map/ppermute | solution.py:12
  155.7 35.1 %collective-permute-start.2 = (f32[128,1024]{0,1:T(8,128)S(1)}, f32[128,1024]{0,1:T(8,128)}, u32[]{:S(2)}, u32[]{:S(2)}) collective-permute-start(f32[128,1024]{0,1:T(8,128)S(1)} %add.137), channel_id=1, source_target_pairs={{0,64},{32,96},{64,0},{96,32},{128,192},{160,224},{192,128},{224,1... | collective-permute-start | bytes 1572872 | tf_op jit(solution)/shard_map/ppermute | solution.py:12
  243.7 39.0 %copy-start.3 = (bf16[1024,896]{1,0:T(8,128)(2,1)}, bf16[1024,896]{1,0:T(8,128)(2,1)S(1)}, u32[]{:S(2)}) copy-start(bf16[1024,896]{1,0:T(8,128)(2,1)S(1)} %add_convert_fusion.1) | copy-start | bytes 5505028
  244.4 12.7 %collective-permute-start.3 = (f32[128,896]{0,1:T(8,128)S(1)}, f32[128,896]{0,1:T(8,128)S(1)}, u32[]{:S(2)}, u32[]{:S(2)}) collective-permute-start(f32[128,896]{0,1:T(8,128)S(1)} %convolution_bitcast_fusion.2), channel_id=1, source_target_pairs={{0,32},{32,0},{64,96},{96,64},{128,160},{160,128},{192,224},{224,1... | collective-permute-start | bytes 1376264 | tf_op jit(solution)/shard_map/ppermute | solution.py:12
  257.1 25.5 %collective-permute-start.4 = (f32[128,896]{0,1:T(8,128)S(1)}, f32[128,896]{0,1:T(8,128)S(1)}, u32[]{:S(2)}, u32[]{:S(2)}) collective-permute-start(f32[128,896]{0,1:T(8,128)S(1)} %add.141), channel_id=1, source_target_pairs={{0,64},{32,96},{64,0},{96,32},{128,192},{160,224},{192,128},{224,1... | collective-permute-start | bytes 1376264 | tf_op jit(solution)/shard_map/ppermute | solution.py:12
  282.7 48.2 %collective-permute-start.5 = (f32[128,896]{0,1:T(8,128)S(1)}, f32[128,896]{0,1:T(8,128)S(1)}, u32[]{:S(2)}, u32[]{:S(2)}) collective-permute-start(f32[128,896]{0,1:T(8,128)S(1)} %add.142), channel_id=1, source_target_pairs={{0,128},{32,160},{64,192},{96,224},{128,0},{160,32},{192,64},{224,... | collective-permute-start | bytes 1376264 | tf_op jit(solution)/shard_map/ppermute | solution.py:12
  382.7 12.1 %collective-permute-start.6 = (f32[128,768]{0,1:T(8,128)S(1)}, f32[128,768]{0,1:T(8,128)S(1)}, u32[]{:S(2)}, u32[]{:S(2)}) collective-permute-start(f32[128,768]{0,1:T(8,128)S(1)} %convolution_bitcast_fusion.3), channel_id=1, source_target_pairs={{0,32},{32,0},{64,96},{96,64},{128,160},{160,128},{192,224},{224,1... | collective-permute-start | bytes 1179656 | tf_op jit(solution)/shard_map/ppermute | solution.py:12
  394.8 22.2 %collective-permute-start.7 = (f32[128,768]{0,1:T(8,128)S(1)}, f32[128,768]{0,1:T(8,128)S(1)}, u32[]{:S(2)}, u32[]{:S(2)}) collective-permute-start(f32[128,768]{0,1:T(8,128)S(1)} %add.146), channel_id=1, source_target_pairs={{0,64},{32,96},{64,0},{96,32},{128,192},{160,224},{192,128},{224,1... | collective-permute-start | bytes 1179656 | tf_op jit(solution)/shard_map/ppermute | solution.py:12
  417.1 40.2 %collective-permute-start.8 = (f32[128,768]{0,1:T(8,128)S(1)}, f32[128,768]{0,1:T(8,128)S(1)}, u32[]{:S(2)}, u32[]{:S(2)}) collective-permute-start(f32[128,768]{0,1:T(8,128)S(1)} %add.147), channel_id=1, source_target_pairs={{0,128},{32,160},{64,192},{96,224},{128,0},{160,32},{192,64},{224,... | collective-permute-start | bytes 1179656 | tf_op jit(solution)/shard_map/ppermute | solution.py:12
  458.1 33.9 %collective-permute-start.9 = (f32[128,768]{0,1:T(8,128)}, f32[128,768]{0,1:T(8,128)}, u32[]{:S(2)}, u32[]{:S(2)}) collective-permute-start(f32[128,768]{0,1:T(8,128)} %add.148), channel_id=1, source_target_pairs={{0,256},{32,288},{64,320},{96,352},{128,384},{160,416},{192,448},{... | collective-permute-start | bytes 1179656 | tf_op jit(solution)/shard_map/ppermute | solution.py:12
  567.1 70.8 %copy-start.4 = (bf16[1024,640]{1,0:T(8,128)(2,1)}, bf16[1024,640]{1,0:T(8,128)(2,1)S(1)}, u32[]{:S(2)}) copy-start(bf16[1024,640]{1,0:T(8,128)(2,1)S(1)} %add_convert_fusion.3) | copy-start | bytes 3932164
  567.6 10.6 %collective-permute-start.10 = (f32[128,640]{0,1:T(8,128)S(1)}, f32[128,640]{0,1:T(8,128)S(1)}, u32[]{:S(2)}, u32[]{:S(2)}) collective-permute-start(f32[128,640]{0,1:T(8,128)S(1)} %convolution_bitcast_fusion.4), channel_id=1, source_target_pairs={{0,32},{32,0},{64,96},{96,64},{128,160},{160,128},{192,224},{224,1... | collective-permute-start | bytes 983048 | tf_op jit(solution)/shard_map/ppermute | solution.py:91
  578.3 24.0 %collective-permute-start.11 = (f32[128,640]{0,1:T(8,128)S(1)}, f32[128,640]{0,1:T(8,128)S(1)}, u32[]{:S(2)}, u32[]{:S(2)}) collective-permute-start(f32[128,640]{0,1:T(8,128)S(1)} %add.152), channel_id=1, source_target_pairs={{0,64},{32,96},{64,0},{96,32},{128,192},{160,224},{192,128},{224,1... | collective-permute-start | bytes 983048 | tf_op jit(solution)/shard_map/ppermute | solution.py:91
  602.3 35.5 %collective-permute-start.12 = (f32[128,640]{0,1:T(8,128)S(1)}, f32[128,640]{0,1:T(8,128)S(1)}, u32[]{:S(2)}, u32[]{:S(2)}) collective-permute-start(f32[128,640]{0,1:T(8,128)S(1)} %add.153), channel_id=1, source_target_pairs={{0,128},{32,160},{64,192},{96,224},{128,0},{160,32},{192,64},{224,... | collective-permute-start | bytes 983048 | tf_op jit(solution)/shard_map/ppermute | solution.py:91
  637.9 36.6 %collective-permute-start.13 = (f32[128,640]{0,1:T(8,128)S(1)}, f32[128,640]{0,1:T(8,128)S(1)}, u32[]{:S(2)}, u32[]{:S(2)}) collective-permute-start(f32[128,640]{0,1:T(8,128)S(1)} %add.154), channel_id=1, source_target_pairs={{0,256},{32,288},{64,320},{96,352},{128,384},{160,416},{192,448},{... | collective-permute-start | bytes 983048 | tf_op jit(solution)/shard_map/ppermute | solution.py:91
  674.5 3.7 collective-permute-start.14
